TPU v7x, 32 devices: a whole 2x2x4 slice. The times are simulated.
32 devices in a mesh: seg: 2 (over y), ch: 16 (over z, x, core).
Axes of the slice: x: 2, y: 2, z: 4, core: 2. Of those that a mesh axis runs over, the one named last changes fastest.
Arguments:
- strain: float32 [2, 1024, 2048], P('seg', 'ch')
- ref_local: int32 [4, 16], replicated, may hold values from 0 to 127, as said below
- owners: int32 [4], replicated, may hold values from 0 to 15, as said below
Outputs:
- toeplitz_blocks: float32 [64, 2048, 64], P('seg', 'ch')
Inputs may be any that keep to these rules, and one draw needn't show every extreme that they name: `ref_local`: each row holds 16 distinct offsets; the first row holds 127. `owners`: the 4 entries are distinct, and one of them is 15.
All inputs are finite; a program needn't handle non-finite values.
Results may differ from a plain program's by a relative error of at most 0.0029.
Values may be sent and summed in bfloat16 or wider, within the bound.
A program may use at most 64 MiB of HBM per device.

v0:
```python
import jax
import jax.numpy as jnp
from jax import lax
from jax.sharding import PartitionSpec as P

L = 64


def spread_2(block, axis, holder):
    block = jnp.where(lax.axis_index(axis) == holder, block, jnp.zeros_like(block))
    return lax.psum(block, axis)


def detrend_cols(series):
    n_total = series.shape[0]
    mid_time = (n_total - 1) / 2.0
    spread = n_total * (n_total * n_total - 1) / 12.0
    centred = (jnp.arange(n_total, dtype=jnp.float32) - mid_time)[:, None]
    level_val = jnp.sum(series, axis=0) / n_total
    slope_val = jnp.sum(centred * series, axis=0) / spread
    return (series - level_val - slope_val * centred).astype(jnp.bfloat16)


def owner_panels(detrended, ref_local, owners):
    pieces = []
    for panel_id in range(ref_local.shape[0]):
        own_cols = jnp.take(detrended, ref_local[panel_id], axis=1)
        pieces.append(spread_2(own_cols, "ch", owners[panel_id]))
    return jnp.concatenate(pieces, axis=1)


def per_device(strain, ref_local, owners):
    my_rows = strain[0]
    s_dev, chans = my_rows.shape
    n_ch = lax.axis_size("ch")
    n_seg = lax.axis_size("seg")
    n_total = s_dev * n_ch
    c_dev = chans // n_ch
    series = lax.all_to_all(my_rows, "ch", split_axis=1, concat_axis=0, tiled=True)
    detrended = detrend_cols(series)
    panels = owner_panels(detrended, ref_local, owners)
    width_ref = panels.shape[1]
    padded = jnp.concatenate([detrended, jnp.zeros((L, c_dev), jnp.bfloat16)], axis=0)
    blk_rows = min(512, n_total)
    n_blocks = n_total // blk_rows
    lag_dev = L // n_seg
    lag_count = lax.axis_size("seg") * lag_dev

    def add_block(blk_idx, running):
        blk_start = blk_idx * blk_rows
        window = lax.dynamic_slice_in_dim(padded, blk_start, blk_rows + lag_count - 1, 0)
        lagged = jnp.concatenate(
            [window[lag_off : lag_off + blk_rows] for lag_off in range(lag_count)], axis=1
        )
        ref_block = lax.dynamic_slice_in_dim(panels, blk_start, blk_rows, 0)
        return running + lax.dot_general(
            lagged, ref_block, (((0,), (0,)), ((), ())), preferred_element_type=jnp.float32
        )

    start_acc = jnp.zeros((lag_count * c_dev, width_ref), jnp.float32)
    running = lax.fori_loop(0, n_blocks, add_block, start_acc)
    summed = lax.psum_scatter(
        running.reshape(lag_count, c_dev, width_ref), "seg", scatter_dimension=0, tiled=True
    )
    lag_ids = (lax.axis_index("seg") * lag_dev + jnp.arange(lag_dev, dtype=jnp.int32)).astype(
        jnp.float32
    )
    return summed / (n_seg * (n_total - lag_ids))[:, None, None]


def solution(mesh):
    in_specs = (P("seg", "ch", None), P(), P())
    out_specs = P("seg", "ch", None)
    return jax.shard_map(
        per_device, mesh=mesh, in_specs=in_specs, out_specs=out_specs, check_vma=False
    )
```

profile of v0, /device:TPU:0, one launch (start us, length us, event | category | flops | bytes accessed | tf_op | source)
XLA Modules:
  0.0 272.1 jit_solution(4993539267196957720)
XLA Ops:
  6.5 1.1 copy.23
  7.7 1.0 copy.16
  8.6 7.4 %all-to-all-start = ((f32[64,16,128]{2,0,1:T(8,128)}), f32[64,16,128]{2,0,1:T(8,128)S(1)}, u32[]{:S(2)}, u32[]{:S(2)}) async-start(f32[64,16,128]{2,0,1:T(8,128)} %copy.16), calls=%async_computation | async-start | bytes 1048576 | tf_op jit(solution)/shard_map/all_to_all | solution.py:39
  16.1 1.5 fusion.3
  20.0 0.8 compare_and_fusion.3
  20.9 9.4 %all-to-all-done = f32[64,16,128]{2,0,1:T(8,128)S(1)} async-done(((f32[64,16,128]{2,0,1:T(8,128)}), f32[64,16,128]{2,0,1:T(8,128)S(1)}, u32[]{:S(2)}, u32[]{:S(2)}) %all-to-all-start) | async-done | bytes 524320 | tf_op jit(solution)/shard_map/all_to_all | solution.py:39
  36.4 88.2 %all-reduce.4.cloned.1.call-done = (bf16[1024,16]{0,1:T(8,128)(2,1)}, bf16[1024,16]{0,1:T(8,128)(2,1)}, bf16[1024,16]{0,1:T(8,128)(2,1)}, bf16[1024,16]{0,1:T(8,128)(2,1)}) async-done(((bf16[1024,16]{0,1:T(8,128)(2,1)}, bf16[1024,16]{0,1:T(8,128)(2,1)}, bf16[1024,16]{0,1:T(8,128)(2,1)}, bf16[1024,16]{0,1:T(8,128)(2,1)}), (bf16[1024,16]{0,1:T(8,128)(2,1)}, bf16[1024,16]{0,1:T(8,128)(2,1)}, ...) | async-done | bytes 131088 | tf_op jit(solution)/shard_map/psum | solution.py:11
  124.6 0.8 pad_maximum_fusion
  125.4 101.3 %while.14 = (s32[]{:T(128)}, f32[8192,64]{0,1:T(8,128)S(1)}, bf16[1088,128]{1,0:T(8,128)(2,1)S(1)}, bf16[1024,64]{0,1:T(8,128)(2,1)S(1)}, s32[]{:T(128)}, /*inde...) while((s32[]{:T(128)}, f32[8192,64]{0,1:T(8,128)S(1)}, ...), condition=%wide.region_7.9_spmd.clone, body=%wide.region_6.8_spmd.clone.sunk | while | flops 537919552 | bytes 29427356 | solution.py:61
  135.3 0.8 constant_dynamic-update-slice_fusion.142
  136.0 0.7 constant_dynamic-update-slice_fusion.143
  143.1 0.7 constant_dynamic-update-slice_fusion.153
  146.7 0.8 constant_dynamic-update-slice_fusion.158
  147.4 0.7 constant_dynamic-update-slice_fusion.159
  150.3 0.8 constant_dynamic-update-slice_fusion.163
  158.1 0.7 constant_dynamic-update-slice_fusion.174
  163.1 0.8 constant_dynamic-update-slice_fusion.181
  164.6 0.7 constant_dynamic-update-slice_fusion.183
  170.9 5.2 %convolution_add_fusion.2 = f32[8192,64]{0,1:T(8,128)S(1)} fusion(bf16[512,8192]{1,0:T(8,128)(2,1)} %constant_dynamic-update-slice_fusion.191, f32[8192,64]{0,1:T(8,128)S(1)} %get-tuple-element.251, pred[]{:T(512)S(6)} %compare.4, bf16[1024,64]{0,1:T(8,128)(2,1)S(1)} %get-tuple-element.325, s32[]{:T(128)S(6)} %select_n.98), kind=kOutput, calls=%fused_computation.4.clone.1 | convolution fusion | flops 537919488 | bytes 12648453 | tf_op jit(solution)/shard_map/while/body/eval_jaxpr/dot_general | solution.py:56
  185.9 0.8 constant_dynamic-update-slice_fusion.142
  186.7 0.7 constant_dynamic-update-slice_fusion.143
  193.7 0.7 constant_dynamic-update-slice_fusion.153
  197.3 0.8 constant_dynamic-update-slice_fusion.158
  198.1 0.7 constant_dynamic-update-slice_fusion.159
  200.9 0.8 constant_dynamic-update-slice_fusion.163
  208.8 0.7 constant_dynamic-update-slice_fusion.174
  213.7 0.8 constant_dynamic-update-slice_fusion.181
  221.5 5.2 %convolution_add_fusion.2 = f32[8192,64]{0,1:T(8,128)S(1)} fusion(bf16[512,8192]{1,0:T(8,128)(2,1)} %constant_dynamic-update-slice_fusion.191, f32[8192,64]{0,1:T(8,128)S(1)} %get-tuple-element.251, pred[]{:T(512)S(6)} %compare.4, bf16[1024,64]{0,1:T(8,128)(2,1)S(1)} %get-tuple-element.325, s32[]{:T(128)S(6)} %select_n.98), kind=kOutput, calls=%fused_computation.4.clone.1 | convolution fusion | flops 537919488 | bytes 12648453 | tf_op jit(solution)/shard_map/while/body/eval_jaxpr/dot_general | solution.py:56
  226.7 1.7 copy.24
  228.5 33.8 %reduce-scatter.2.cloned.1.call-done = f32[32,128,64]{1,0,2:T(8,128)} async-done(((f32[64,128,64]{1,0,2:T(8,128)}), f32[32,128,64]{1,0,2:T(8,128)}) %reduce-scatter.2.cloned.1.call-update) | async-done | bytes 1048592 | tf_op jit(solution)/shard_map/reduce_scatter | solution.py:62
  262.3 1.4 broadcast_divide_fusion
  263.7 1.6 copy.20
  (136 shorter events, 84.3 us)
Async XLA Ops:
  8.6 21.7 %all-to-all-start = ((f32[64,16,128]{2,0,1:T(8,128)}), f32[64,16,128]{2,0,1:T(8,128)S(1)}, u32[]{:S(2)}, u32[]{:S(2)}) async-start(f32[64,16,128]{2,0,1:T(8,128)} %copy.16), calls=%async_computation | async-start | bytes 1048576 | tf_op jit(solution)/shard_map/all_to_all | solution.py:39
  16.0 108.6 %all-reduce.4.cloned.1.call-start = ((), (), s32[]{:S(2)}) async-start(), calls=%async_computation.3 | async-start | bytes 262144 | tf_op jit(solution)/shard_map/psum | solution.py:11
  36.2 226.1 %reduce-scatter.2.cloned.1.call-start = ((), (), s32[]{:S(2)}) async-start(), calls=%async_computation.2 | async-start | bytes 3145728 | tf_op jit(solution)/shard_map/reduce_scatter | solution.py:62
Sparse Core Ops, SparseCore 0:
  36.3 88.2 all-reduce.3
  228.6 33.6 reduce-scatter.1
where the time goes:
time: 273 us; the launch traced here: 272 us
  waiting for transfers between devices  131 us (48%)
  local copies, waits for them, and re-layouts  100 us (37%)
  between operations  16 us (6%)
  matrix products  10.4 us (4%)
  starting transfers between devices  7.47 us (3%)
  other arithmetic  6.38 us (2%)
    while x126, local copies, waits for them, and re-layouts  89.4 us
    psum x1, waiting for transfers between devices, spread_2(): return lax.psum(block, axis)  88.2 us
    reduce_scatter x1, waiting for transfers between devices, per_device(): lax.psum_scatter(running.reshape(lag_count, c_dev, width_ref), 'seg', sca...  33.8 us
    dot_general x2, matrix products, add_block(): lax.dot_general(lagged, ref_block, (((0,), (0,)), ((), ())), preferred_el...  10.4 us
    all_to_all x1, waiting for transfers between devices, per_device(): lax.all_to_all(my_rows, 'ch', split_axis=1, concat_axis=0, tiled=True)  9.4 us
    all_to_all x1, starting transfers between devices, per_device(): lax.all_to_all(my_rows, 'ch', split_axis=1, concat_axis=0, tiled=True)  7.39 us
  transfers between devices with their start and end apart: 3, of which 3 were waited for; matrix products, arithmetic and copies ran while one was open for 1% of the time, Pallas kernels for 0%

commit v1 on v0

--- a/solution.py
+++ b/solution.py
@@ -4,6 +4,18 @@
 from jax.sharding import PartitionSpec as P
 
 L = 64
+
+
+def in_blocks(shard, dim, length):
+    lengths = shard.shape
+    blocks = shard.reshape(*lengths[:dim], length, lengths[dim] // length, *lengths[dim + 1 :])
+    return jnp.moveaxis(blocks, dim, 0)
+
+
+def in_order(blocks, dim):
+    blocks = jnp.moveaxis(blocks, 0, dim)
+    lengths = blocks.shape
+    return blocks.reshape(*lengths[:dim], lengths[dim] * lengths[dim + 1], *lengths[dim + 2 :])
 
 
 def spread_2(block, axis, holder):
@@ -36,7 +48,15 @@
     n_seg = lax.axis_size("seg")
     n_total = s_dev * n_ch
     c_dev = chans // n_ch
-    series = lax.all_to_all(my_rows, "ch", split_axis=1, concat_axis=0, tiled=True)
+    size, here = (lax.axis_size("ch"), lax.axis_index("ch"))
+    blocks = in_blocks(my_rows, 1, size)
+    whole = blocks
+    for step in range(1, size):
+        target, source = ((here + step) % size, (here - step) % size)
+        sent = lax.dynamic_index_in_dim(blocks, target, 0)
+        other = lax.ppermute(sent, "ch", [(i, (i + step) % size) for i in range(size)])
+        whole = lax.dynamic_update_slice_in_dim(whole, other, source, axis=0)
+    series = in_order(whole, 0)
     detrended = detrend_cols(series)
     panels = owner_panels(detrended, ref_local, owners)
     width_ref = panels.shape[1]

time: 273 us -> 281 us (1.029)
  starting transfers between devices: 7.47 us -> 24.5 us
  waiting for transfers between devices: 131 us -> 120 us
    ppermute x0 -> x15, starting transfers between devices: none -> 24.3 us  [per_device(): lax.ppermute(sent, 'ch', [(i, (i + step) % size) for i in range(size)])]
    all_to_all x1 -> x0, waiting for transfers between devices: 9.4 us -> none  [per_device(): lax.all_to_all(my_rows, 'ch', split_axis=1, concat_axis=0, tiled=True)]
    all_to_all x1 -> x0, starting transfers between devices: 7.39 us -> none  [per_device(): lax.all_to_all(my_rows, 'ch', split_axis=1, concat_axis=0, tiled=True)]
  transfers between devices with their start and end apart: 3 -> 17, of which waited for: 3 -> 2; matrix products, arithmetic and copies ran while one was open for 1% -> 2% of each run, Pallas kernels for 0% -> 0%
where the time goes in v1:
time: 281 us; the launch traced here: 280 us
  waiting for transfers between devices  120 us (43%)
  local copies, waits for them, and re-layouts  102 us (36%)
  starting transfers between devices  24.5 us (9%)
  between operations  16.3 us (6%)
  matrix products  10.4 us (4%)
  other arithmetic  6.2 us (2%)
    while x126, local copies, waits for them, and re-layouts  89.3 us
    psum x1, waiting for transfers between devices, spread_2(): return lax.psum(block, axis)  86.4 us
    reduce_scatter x1, waiting for transfers between devices, per_device(): lax.psum_scatter(running.reshape(lag_count, c_dev, width_ref), 'seg', sca...  33.8 us
    ppermute x15, starting transfers between devices, per_device(): lax.ppermute(sent, 'ch', [(i, (i + step) % size) for i in range(size)])  24.3 us
    dot_general x2, matrix products, add_block(): lax.dot_general(lagged, ref_block, (((0,), (0,)), ((), ())), preferred_el...  10.4 us
  transfers between devices with their start and end apart: 17, of which 2 were waited for; matrix products, arithmetic and copies ran while one was open for 2% of the time, Pallas kernels for 0%

profile of v1, /device:TPU:0, one launch (start us, length us, event | category | flops | bytes accessed | tf_op | source)
XLA Modules:
  0.0 280.1 jit_solution(16589553328245704945)
XLA Ops:
  6.5 1.1 copy.33
  8.8 2.5 collective-permute-start.1
  11.3 2.4 collective-permute-start.2
  13.7 1.6 collective-permute-start.3
  15.5 0.8 compare_and_fusion.3
  16.4 1.5 fusion.3
  17.9 1.3 collective-permute-start.5
  19.1 4.3 %collective-permute-start.6 = (f32[1,64,128]{2,0,1:T(1,128)S(1)}, f32[1,64,128]{2,0,1:T(1,128)S(1)}, u32[]{:S(2)}, u32[]{:S(2)}) collective-permute-start(f32[1,64,128]{2,0,1:T(1,128)S(1)} %get-tuple-element.143), channel_id=1, source_target_pairs={{0,7},{1,8},{2,9},{3,10},{4,11},{5,12},{6,13},{7,14},{8,15},{9,0},... | collective-permute-start | bytes 98312 | tf_op jit(solution)/shard_map/ppermute | solution.py:57
  24.1 2.4 collective-permute-start.9
  26.5 2.9 %collective-permute-start.10 = (f32[1,64,128]{2,0,1:T(1,128)S(1)}, f32[1,64,128]{2,0,1:T(1,128)S(1)}, u32[]{:S(2)}, u32[]{:S(2)}) collective-permute-start(f32[1,64,128]{2,0,1:T(1,128)S(1)} %get-tuple-element.139), channel_id=1, source_target_pairs={{0,11},{1,12},{2,13},{3,14},{4,15},{5,0},{6,1},{7,2},{8,3},{9,4},{... | collective-permute-start | bytes 98312 | tf_op jit(solution)/shard_map/ppermute | solution.py:57
  29.4 1.8 collective-permute-start.11
  31.2 1.5 collective-permute-start.13
  32.7 2.2 collective-permute-start.14
  46.2 86.4 %all-reduce.4.cloned.1.call-done = (bf16[1024,16]{0,1:T(8,128)(2,1)}, bf16[1024,16]{0,1:T(8,128)(2,1)}, bf16[1024,16]{0,1:T(8,128)(2,1)}, bf16[1024,16]{0,1:T(8,128)(2,1)}) async-done(((bf16[1024,16]{0,1:T(8,128)(2,1)}, bf16[1024,16]{0,1:T(8,128)(2,1)}, bf16[1024,16]{0,1:T(8,128)(2,1)}, bf16[1024,16]{0,1:T(8,128)(2,1)}), (bf16[1024,16]{0,1:T(8,128)(2,1)}, bf16[1024,16]{0,1:T(8,128)(2,1)}, ...) | async-done | bytes 131088 | tf_op jit(solution)/shard_map/psum | solution.py:23
  132.6 0.8 pad_maximum_fusion
  133.4 101.3 %while.14 = (s32[]{:T(128)}, f32[8192,64]{0,1:T(8,128)S(1)}, bf16[1088,128]{1,0:T(8,128)(2,1)S(1)}, bf16[1024,64]{0,1:T(8,128)(2,1)S(1)}, s32[]{:T(128)}, /*inde...) while((s32[]{:T(128)}, f32[8192,64]{0,1:T(8,128)S(1)}, ...), condition=%wide.region_7.9_spmd.clone, body=%wide.region_6.8_spmd.clone.sunk | while | flops 537919552 | bytes 29427356 | solution.py:81
  148.8 0.7 constant_dynamic-update-slice_fusion.150
  160.3 0.7 constant_dynamic-update-slice_fusion.166
  161.0 0.7 constant_dynamic-update-slice_fusion.167
  163.9 0.8 constant_dynamic-update-slice_fusion.171
  176.7 0.7 constant_dynamic-update-slice_fusion.189
  178.8 5.2 %convolution_add_fusion.2 = f32[8192,64]{0,1:T(8,128)S(1)} fusion(bf16[512,8192]{1,0:T(8,128)(2,1)} %constant_dynamic-update-slice_fusion.191, f32[8192,64]{0,1:T(8,128)S(1)} %get-tuple-element.264, pred[]{:T(512)S(6)} %compare.34, bf16[1024,64]{0,1:T(8,128)(2,1)S(1)} %get-tuple-element.338, s32[]{:T(128)S(6)} %select_n.372), kind=kOutput, calls=%fused_computation.4.clone.1 | convolution fusion | flops 537919488 | bytes 12648453 | tf_op jit(solution)/shard_map/while/body/eval_jaxpr/dot_general | solution.py:76
  199.4 0.7 constant_dynamic-update-slice_fusion.150
  210.9 0.7 constant_dynamic-update-slice_fusion.166
  211.6 0.7 constant_dynamic-update-slice_fusion.167
  214.5 0.8 constant_dynamic-update-slice_fusion.171
  227.3 0.7 constant_dynamic-update-slice_fusion.189
  229.5 5.2 %convolution_add_fusion.2 = f32[8192,64]{0,1:T(8,128)S(1)} fusion(bf16[512,8192]{1,0:T(8,128)(2,1)} %constant_dynamic-update-slice_fusion.191, f32[8192,64]{0,1:T(8,128)S(1)} %get-tuple-element.264, pred[]{:T(512)S(6)} %compare.34, bf16[1024,64]{0,1:T(8,128)(2,1)S(1)} %get-tuple-element.338, s32[]{:T(128)S(6)} %select_n.372), kind=kOutput, calls=%fused_computation.4.clone.1 | convolution fusion | flops 537919488 | bytes 12648453 | tf_op jit(solution)/shard_map/while/body/eval_jaxpr/dot_general | solution.py:76
  234.7 1.7 copy.34
  236.4 33.8 %reduce-scatter.2.cloned.1.call-done = f32[32,128,64]{1,0,2:T(8,128)} async-done(((f32[64,128,64]{1,0,2:T(8,128)}), f32[32,128,64]{1,0,2:T(8,128)}) %reduce-scatter.2.cloned.1.call-update) | async-done | bytes 1048592 | tf_op jit(solution)/shard_map/reduce_scatter | solution.py:82
  270.2 1.4 broadcast_divide_fusion
  271.7 1.6 copy.30
  (179 shorter events, 93.7 us)
Async XLA Ops:
  6.5 126.1 %all-reduce.4.cloned.1.call-start = ((), (), s32[]{:S(2)}) async-start(), calls=%async_computation.2 | async-start | bytes 262144 | tf_op jit(solution)/shard_map/psum | solution.py:23
  8.2 9.6 %collective-permute-start = (f32[1,64,128]{2,0,1:T(1,128)S(1)}, f32[1,64,128]{2,0,1:T(1,128)S(1)}, u32[]{:S(2)}, u32[]{:S(2)}) collective-permute-start(f32[1,64,128]{2,0,1:T(1,128)S(1)} %get-tuple-element.149), channel_id=1, source_target_pairs={{0,1},{1,2},{2,3},{3,4},{4,5},{5,6},{6,7},{7,8},{8,9},{9,10},{10,1... | collective-permute-start | bytes 98312 | tf_op jit(solution)/shard_map/ppermute | solution.py:57
  8.8 10.3 %collective-permute-start.1 = (f32[1,64,128]{2,0,1:T(1,128)S(1)}, f32[1,64,128]{2,0,1:T(1,128)S(1)}, u32[]{:S(2)}, u32[]{:S(2)}) collective-permute-start(f32[1,64,128]{2,0,1:T(1,128)S(1)} %get-tuple-element.148), channel_id=1, source_target_pairs={{0,2},{1,3},{2,4},{3,5},{4,6},{5,7},{6,8},{7,9},{8,10},{9,11},{10,... | collective-permute-start | bytes 98312 | tf_op jit(solution)/shard_map/ppermute | solution.py:57
  11.3 12.1 %collective-permute-start.2 = (f32[1,64,128]{2,0,1:T(1,128)S(1)}, f32[1,64,128]{2,0,1:T(1,128)S(1)}, u32[]{:S(2)}, u32[]{:S(2)}) collective-permute-start(f32[1,64,128]{2,0,1:T(1,128)S(1)} %get-tuple-element.147), channel_id=1, source_target_pairs={{0,3},{1,4},{2,5},{3,6},{4,7},{5,8},{6,9},{7,10},{8,11},{9,12},{10... | collective-permute-start | bytes 98312 | tf_op jit(solution)/shard_map/ppermute | solution.py:57
  13.7 10.0 %collective-permute-start.3 = (f32[1,64,128]{2,0,1:T(1,128)S(1)}, f32[1,64,128]{2,0,1:T(1,128)S(1)}, u32[]{:S(2)}, u32[]{:S(2)}) collective-permute-start(f32[1,64,128]{2,0,1:T(1,128)S(1)} %get-tuple-element.146), channel_id=1, source_target_pairs={{0,4},{1,5},{2,6},{3,7},{4,8},{5,9},{6,10},{7,11},{8,12},{9,13},{1... | collective-permute-start | bytes 98312 | tf_op jit(solution)/shard_map/ppermute | solution.py:57
  15.3 8.8 %collective-permute-start.4 = (f32[1,64,128]{2,0,1:T(1,128)S(1)}, f32[1,64,128]{2,0,1:T(1,128)S(1)}, u32[]{:S(2)}, u32[]{:S(2)}) collective-permute-start(f32[1,64,128]{2,0,1:T(1,128)S(1)} %get-tuple-element.145), channel_id=1, source_target_pairs={{0,5},{1,6},{2,7},{3,8},{4,9},{5,10},{6,11},{7,12},{8,13},{9,14},{... | collective-permute-start | bytes 98312 | tf_op jit(solution)/shard_map/ppermute | solution.py:57
  17.9 8.6 %collective-permute-start.5 = (f32[1,64,128]{2,0,1:T(1,128)S(1)}, f32[1,64,128]{2,0,1:T(1,128)S(1)}, u32[]{:S(2)}, u32[]{:S(2)}) collective-permute-start(f32[1,64,128]{2,0,1:T(1,128)S(1)} %get-tuple-element.144), channel_id=1, source_target_pairs={{0,6},{1,7},{2,8},{3,9},{4,10},{5,11},{6,12},{7,13},{8,14},{9,15},... | collective-permute-start | bytes 98312 | tf_op jit(solution)/shard_map/ppermute | solution.py:57
  19.1 10.3 %collective-permute-start.6 = (f32[1,64,128]{2,0,1:T(1,128)S(1)}, f32[1,64,128]{2,0,1:T(1,128)S(1)}, u32[]{:S(2)}, u32[]{:S(2)}) collective-permute-start(f32[1,64,128]{2,0,1:T(1,128)S(1)} %get-tuple-element.143), channel_id=1, source_target_pairs={{0,7},{1,8},{2,9},{3,10},{4,11},{5,12},{6,13},{7,14},{8,15},{9,0},... | collective-permute-start | bytes 98312 | tf_op jit(solution)/shard_map/ppermute | solution.py:57
  23.5 7.8 %collective-permute-start.7 = (f32[1,64,128]{2,0,1:T(1,128)S(1)}, f32[1,64,128]{2,0,1:T(1,128)S(1)}, u32[]{:S(2)}, u32[]{:S(2)}) collective-permute-start(f32[1,64,128]{2,0,1:T(1,128)S(1)} %get-tuple-element.142), channel_id=1, source_target_pairs={{0,8},{1,9},{2,10},{3,11},{4,12},{5,13},{6,14},{7,15},{8,0},{9,1},... | collective-permute-start | bytes 98312 | tf_op jit(solution)/shard_map/ppermute | solution.py:57
  23.8 7.4 %collective-permute-start.8 = (f32[1,64,128]{2,0,1:T(1,128)S(1)}, f32[1,64,128]{2,0,1:T(1,128)S(1)}, u32[]{:S(2)}, u32[]{:S(2)}) collective-permute-start(f32[1,64,128]{2,0,1:T(1,128)S(1)} %get-tuple-element.141), channel_id=1, source_target_pairs={{0,9},{1,10},{2,11},{3,12},{4,13},{5,14},{6,15},{7,0},{8,1},{9,2},... | collective-permute-start | bytes 98312 | tf_op jit(solution)/shard_map/ppermute | solution.py:57
  24.1 8.6 %collective-permute-start.9 = (f32[1,64,128]{2,0,1:T(1,128)S(1)}, f32[1,64,128]{2,0,1:T(1,128)S(1)}, u32[]{:S(2)}, u32[]{:S(2)}) collective-permute-start(f32[1,64,128]{2,0,1:T(1,128)S(1)} %get-tuple-element.140), channel_id=1, source_target_pairs={{0,10},{1,11},{2,12},{3,13},{4,14},{5,15},{6,0},{7,1},{8,2},{9,3},... | collective-permute-start | bytes 98312 | tf_op jit(solution)/shard_map/ppermute | solution.py:57
  26.5 12.6 %collective-permute-start.10 = (f32[1,64,128]{2,0,1:T(1,128)S(1)}, f32[1,64,128]{2,0,1:T(1,128)S(1)}, u32[]{:S(2)}, u32[]{:S(2)}) collective-permute-start(f32[1,64,128]{2,0,1:T(1,128)S(1)} %get-tuple-element.139), channel_id=1, source_target_pairs={{0,11},{1,12},{2,13},{3,14},{4,15},{5,0},{6,1},{7,2},{8,3},{9,4},{... | collective-permute-start | bytes 98312 | tf_op jit(solution)/shard_map/ppermute | solution.py:57
  29.4 9.8 %collective-permute-start.11 = (f32[1,64,128]{2,0,1:T(1,128)S(1)}, f32[1,64,128]{2,0,1:T(1,128)S(1)}, u32[]{:S(2)}, u32[]{:S(2)}) collective-permute-start(f32[1,64,128]{2,0,1:T(1,128)S(1)} %get-tuple-element.138), channel_id=1, source_target_pairs={{0,12},{1,13},{2,14},{3,15},{4,0},{5,1},{6,2},{7,3},{8,4},{9,5},{1... | collective-permute-start | bytes 98312 | tf_op jit(solution)/shard_map/ppermute | solution.py:57
  31.2 8.2 %collective-permute-start.12 = (f32[1,64,128]{2,0,1:T(1,128)S(1)}, f32[1,64,128]{2,0,1:T(1,128)S(1)}, u32[]{:S(2)}, u32[]{:S(2)}) collective-permute-start(f32[1,64,128]{2,0,1:T(1,128)S(1)} %get-tuple-element.137), channel_id=1, source_target_pairs={{0,13},{1,14},{2,15},{3,0},{4,1},{5,2},{6,3},{7,4},{8,5},{9,6},{10... | collective-permute-start | bytes 98312 | tf_op jit(solution)/shard_map/ppermute | solution.py:57
  31.2 8.3 %collective-permute-start.13 = (f32[1,64,128]{2,0,1:T(1,128)S(1)}, f32[1,64,128]{2,0,1:T(1,128)S(1)}, u32[]{:S(2)}, u32[]{:S(2)}) collective-permute-start(f32[1,64,128]{2,0,1:T(1,128)S(1)} %get-tuple-element.136), channel_id=1, source_target_pairs={{0,14},{1,15},{2,0},{3,1},{4,2},{5,3},{6,4},{7,5},{8,6},{9,7},{10,... | collective-permute-start | bytes 98312 | tf_op jit(solution)/shard_map/ppermute | solution.py:57
  32.7 7.0 %collective-permute-start.14 = (f32[1,64,128]{2,0,1:T(1,128)S(1)}, f32[1,64,128]{2,0,1:T(1,128)S(1)}, u32[]{:S(2)}, u32[]{:S(2)}) collective-permute-start(f32[1,64,128]{2,0,1:T(1,128)S(1)} %get-tuple-element.135), channel_id=1, source_target_pairs={{0,15},{1,0},{2,1},{3,2},{4,3},{5,4},{6,5},{7,6},{8,7},{9,8},{10,9... | collective-permute-start | bytes 98312 | tf_op jit(solution)/shard_map/ppermute | solution.py:57
  45.7 224.5 %reduce-scatter.2.cloned.1.call-start = ((), (), s32[]{:S(2)}) async-start(), calls=%async_computation.1 | async-start | bytes 3145728 | tf_op jit(solution)/shard_map/reduce_scatter | solution.py:82
Sparse Core Ops, SparseCore 0:
  45.9 86.6 all-reduce.3
  236.5 33.6 reduce-scatter.1
